TPU v7x, 128 devices: a whole 4x4x4 slice. The times are simulated.
128 devices in a mesh: seq: 16 (over z, y_hi, core), col: 4 (over x), batch: 2 (over y_lo).
Axes of the slice: x: 4, y: 4 (y_hi: 2, y_lo: 2; y = y_hi * 2 + y_lo), z: 4, core: 2. Of those that a mesh axis runs over, the one named last changes fastest.
Arguments:
- tokens: int32 [2, 1048576], P('batch', ('seq', 'col')), may hold values from 0 to 3
- stem_weight: bfloat16 [64, 768], replicated, may hold values from -1.5 to 1.5
- conv_weight: bfloat16 [3840, 768], replicated, may hold values from -0.09375 to 0.09375
- conv_bias: float32 [768], replicated, may hold values from -1 to 1
- up_weight: bfloat16 [768, 1536], replicated, may hold values from -0.21875 to 0.21875
- norm_gain: float32 [1536], replicated, may hold values from 0.1 to 1.9
- pair_weight: bfloat16 [1536, 64], replicated, may hold values from -0.15625 to 0.15625
- out_weight: bfloat16 [1024, 128], replicated, may hold values from -0.1875 to 0.1875
- cotangent: bfloat16 [2, 512, 512, 128], P('batch', 'seq', 'col'), may hold values from -24 to 24
- projection: float32 [768, 128], replicated, may hold values from -0.21875 to 0.21875
- buckets: int32 [3840], replicated, may hold values from 0 to 31
Outputs:
- input_grad: bfloat16 [2, 65536, 768], P('batch', ('seq', 'col'))
- embedding: float32 [2, 32, 128], P('batch')
All inputs are finite; a program needn't handle non-finite values.
Results may differ from a plain program's by a relative error of at most 0.012.
Values may be sent and summed in bfloat16 or wider, within the bound.
No kernel may reach another device: no remote copies, remote signals or barrier semaphores. Data moves between devices by JAX's collectives and lax.ppermute only.
A program may use at most 128 MiB of HBM per device.

v0:
```python
import jax
import jax.numpy as jnp
from jax import lax
from jax.sharding import PartitionSpec as P

OP = 32
PATCH = 16
POOL = 128
BUCKETS = 32
highest = lax.Precision.HIGHEST


def extended(cells, sides, width):
    for axis, dim in sides:
        count = lax.axis_size(axis)
        ends = count - 1
        head = lax.slice_in_dim(cells, 0, width, axis=dim)
        tail = lax.slice_in_dim(cells, cells.shape[dim] - width, cells.shape[dim], axis=dim)
        cells = jnp.concatenate(
            [
                lax.ppermute(tail, axis, [(i, (i + 1) % count) for i in range(ends)]),
                cells,
                lax.ppermute(head, axis, [((i + 1) % count, i) for i in range(ends)]),
            ],
            axis=dim,
        )
    return cells


def shards(
    tokens,
    stem_weight,
    conv_weight,
    conv_bias,
    up_weight,
    norm_gain,
    pair_weight,
    out_weight,
    cotangent,
    projection,
    buckets,
):
    channels = conv_weight.shape[1]
    kernel = conv_weight.shape[0] // channels
    reach = (kernel - 1) // 2
    patches = tokens.shape[1] // PATCH
    bins_dev = patches // POOL
    bases = tokens[0].reshape(patches, PATCH)
    onehot = (
        (bases[:, :, None] == jnp.arange(4, dtype=jnp.int32))
        .astype(jnp.bfloat16)
        .reshape(patches, PATCH * 4)
    )
    embedded = jnp.dot(onehot, stem_weight, preferred_element_type=jnp.float32).astype(jnp.bfloat16)
    padded = extended(embedded, ((("seq", "col"), 0),), reach)
    unfolded = jnp.concatenate(
        [padded[offset : offset + patches] for offset in range(kernel)], axis=1
    )
    before = jnp.dot(unfolded, conv_weight, preferred_element_type=jnp.float32) + conv_bias
    after, gelu_back = jax.vjp(jax.nn.gelu, before)
    pooled = jnp.mean(after.reshape(bins_dev, POOL, channels), axis=1).astype(jnp.bfloat16)
    hidden = jnp.dot(pooled, up_weight, preferred_element_type=jnp.float32)
    inverse = lax.rsqrt(jnp.mean(hidden * hidden, axis=1, keepdims=True) + 1e-06)
    normed = (hidden * inverse * norm_gain).astype(jnp.bfloat16)
    seq_count = lax.axis_size("seq")
    col_count = lax.axis_size("col")
    row_len = bins_dev * col_count
    col_len = bins_dev * seq_count
    all_bins = row_len * seq_count
    row_index = lax.axis_index("seq")
    col_index = lax.axis_index("col")
    every = lax.all_gather(normed, ("seq", "col"), axis=0, tiled=True)
    row_part = lax.dynamic_slice_in_dim(every, row_index * row_len, row_len, 0)
    col_part = lax.dynamic_slice_in_dim(every, col_index * col_len, col_len, 0)
    left = jnp.dot(row_part, pair_weight[:, :OP], preferred_element_type=jnp.float32).astype(
        jnp.bfloat16
    )
    right = jnp.dot(col_part, pair_weight[:, OP:], preferred_element_type=jnp.float32).astype(
        jnp.bfloat16
    )
    pair_channels = cotangent.shape[3]
    blocks = cotangent[0].reshape(col_count, bins_dev, col_len, pair_channels)
    left_groups = left.astype(jnp.float32).reshape(col_count, bins_dev, OP)
    right_wide = right.astype(jnp.float32)

    def pair_step(carry, inputs):
        block, rows_left = inputs
        outer_grad = lax.dot_general(
            block.reshape(bins_dev * col_len, pair_channels),
            out_weight,
            (((1,), (1,)), ((), ())),
            preferred_element_type=jnp.float32,
        ).reshape(bins_dev, col_len, OP, OP)
        grad_left = jnp.einsum("ijkl,jl->ik", outer_grad, right_wide, precision=highest)
        carry = carry + jnp.einsum("ijkl,ik->jl", outer_grad, rows_left, precision=highest)
        return (carry, grad_left)

    grad_right, grad_left = lax.scan(
        pair_step, jnp.zeros((col_len, OP), jnp.float32), (blocks, left_groups)
    )
    grad_left = grad_left.reshape(row_len, OP)
    row_term = lax.dot_general(
        grad_left,
        pair_weight[:, :OP].astype(jnp.float32),
        (((1,), (1,)), ((), ())),
        precision=highest,
    )
    col_term = lax.dot_general(
        grad_right,
        pair_weight[:, OP:].astype(jnp.float32),
        (((1,), (1,)), ((), ())),
        precision=highest,
    )
    empty_rows = jnp.zeros((all_bins, row_term.shape[1]), jnp.float32)
    placed = lax.dynamic_update_slice_in_dim(
        empty_rows, row_term, row_index * row_len, 0
    ) + lax.dynamic_update_slice_in_dim(empty_rows, col_term, col_index * col_len, 0)
    d_normed = lax.psum_scatter(placed, ("seq", "col"), scatter_dimension=0, tiled=True)
    scaled = d_normed * norm_gain
    inner = jnp.mean(scaled * hidden, axis=1, keepdims=True)
    d_hidden = inverse * scaled - hidden * inverse**3 * inner
    d_pooled = lax.dot_general(
        d_hidden, up_weight.astype(jnp.float32), (((1,), (1,)), ((), ())), precision=highest
    )
    spread = jnp.broadcast_to(d_pooled[:, None, :] / POOL, (bins_dev, POOL, channels)).reshape(
        patches, channels
    )
    d_before = gelu_back(spread)[0].astype(jnp.bfloat16)
    grads_padded = extended(d_before, ((("seq", "col"), 0),), reach)
    stacked = jnp.stack(
        [
            grads_padded[2 * reach - offset : 2 * reach - offset + patches]
            for offset in range(kernel)
        ],
        axis=1,
    )
    input_grad = jnp.einsum(
        "tko,kio->ti",
        stacked,
        conv_weight.reshape(kernel, channels, channels),
        preferred_element_type=jnp.float32,
    ).astype(jnp.bfloat16)
    share_rows = unfolded.shape[1] // lax.axis_size(("seq", "col"))
    share = lax.psum_scatter(
        lax.dot_general(
            unfolded, d_before, (((0,), (0,)), ((), ())), preferred_element_type=jnp.float32
        ),
        ("seq", "col"),
        scatter_dimension=0,
        tiled=True,
    )
    labels = lax.dynamic_slice_in_dim(
        buckets, lax.axis_index(("seq", "col")) * share_rows, share_rows, 0
    )
    projected = jnp.dot(share, projection, precision=highest)
    member = (labels[None, :] == jnp.arange(BUCKETS, dtype=jnp.int32)[:, None]).astype(jnp.float32)
    sketch = lax.psum(jnp.dot(member, projected, precision=highest), ("seq", "col"))
    unit = sketch * lax.rsqrt(jnp.mean(sketch * sketch) + 1e-06)
    center = lax.psum(unit, "batch") / lax.axis_size("batch")
    return (input_grad[None], (unit - center)[None])


def solution(mesh):
    in_specs = (
        P("batch", ("seq", "col")),
        P(),
        P(),
        P(),
        P(),
        P(),
        P(),
        P(),
        P("batch", "seq", "col", None),
        P(),
        P(),
    )
    out_specs = (P("batch", ("seq", "col"), None), P("batch", None, None))
    return jax.shard_map(shards, mesh=mesh, in_specs=in_specs, out_specs=out_specs, check_vma=False)
```

profile of v0, /device:TPU:8, one launch (start us, length us, event | category | flops | bytes accessed | tf_op | source)
XLA Modules:
  0.0 925.7 jit_solution(1880735338173199356)
XLA Ops:
  11.8 3.4 collective-permute-start
  21.5 8.4 bitcast_reduce_fusion
  31.4 72.0 %all-gather.2.cloned.1.call-done = bf16[512,1536]{1,0:T(8,128)(2,1)} async-done(((bf16[8,1536]{1,0:T(8,128)(2,1)}), bf16[512,1536]{1,0:T(8,128)(2,1)}) %all-gather.2.cloned.1.call-update) | async-done | bytes 1572880 | tf_op jit(solution)/shard_map/all_gather | solution.py:72
  105.8 78.4 %while.13 = (s32[]{:T(128)}, f32[128,32]{1,0:T(8,128)S(1)}, f32[4,8,32]{2,1,0:T(8,128)S(1)}, bf16[4,8,128,128]{3,2,1,0:T(8,128)(2,1)}, bf16[1024,128]{1,0:T(8,12...) while((s32[]{:T(128)}, f32[128,32]{1,0:T(8,128)S(1)}, ...), condition=%wide.region_3.4_spmd.clone, body=%wide.region_2.3_spmd.clone.sunk | while | flops 293609472 | bytes 30050948 | solution.py:98
  105.8 3.6 fusion.101
  109.5 11.1 %fusion.102 = f32[1,8,32,1]{2,0,3,1:T(1,128)S(1)} fusion(f32[128,32,1,1]{0,2,1,3:T(1,128)S(1)} %copy.35, f32[8,128,32,32]{1,3,2,0:T(8,128)} %fusion.101), kind=kOutput, calls=%fused_computation.clone.1 | convolution fusion | flops 12582912 | bytes 4211712 | tf_op jit(solution)/shard_map/while/body/eval_jaxpr/ijkl,jl->ik/dot_general | solution.py:94
  120.6 4.7 fusion.103
  125.4 3.6 fusion.101
  129.1 11.1 %fusion.102 = f32[1,8,32,1]{2,0,3,1:T(1,128)S(1)} fusion(f32[128,32,1,1]{0,2,1,3:T(1,128)S(1)} %copy.35, f32[8,128,32,32]{1,3,2,0:T(8,128)} %fusion.101), kind=kOutput, calls=%fused_computation.clone.1 | convolution fusion | flops 12582912 | bytes 4211712 | tf_op jit(solution)/shard_map/while/body/eval_jaxpr/ijkl,jl->ik/dot_general | solution.py:94
  140.2 4.7 fusion.103
  145.0 3.6 fusion.101
  148.7 11.1 %fusion.102 = f32[1,8,32,1]{2,0,3,1:T(1,128)S(1)} fusion(f32[128,32,1,1]{0,2,1,3:T(1,128)S(1)} %copy.35, f32[8,128,32,32]{1,3,2,0:T(8,128)} %fusion.101), kind=kOutput, calls=%fused_computation.clone.1 | convolution fusion | flops 12582912 | bytes 4211712 | tf_op jit(solution)/shard_map/while/body/eval_jaxpr/ijkl,jl->ik/dot_general | solution.py:94
  159.8 4.7 fusion.103
  164.6 3.6 fusion.101
  168.3 11.1 %fusion.102 = f32[1,8,32,1]{2,0,3,1:T(1,128)S(1)} fusion(f32[128,32,1,1]{0,2,1,3:T(1,128)S(1)} %copy.35, f32[8,128,32,32]{1,3,2,0:T(8,128)} %fusion.101), kind=kOutput, calls=%fused_computation.clone.1 | convolution fusion | flops 12582912 | bytes 4211712 | tf_op jit(solution)/shard_map/while/body/eval_jaxpr/ijkl,jl->ik/dot_general | solution.py:94
  179.4 4.7 fusion.103
  191.7 143.6 %reduce-scatter.4.cloned.1.call-done = f32[8,1536]{1,0:T(8,128)} async-done(((f32[512,1536]{1,0:T(8,128)}), f32[8,1536]{1,0:T(8,128)}) %reduce-scatter.4.cloned.1.call-update) | async-done | bytes 49168 | tf_op jit(solution)/shard_map/reduce_scatter | solution.py:118
  339.0 3.7 fusion.15
  342.7 12.6 %fusion.70 = f32[3840,768]{1,0:T(8,128)} fusion(bf16[1024,3840]{1,0:T(8,128)(2,1)} %copy-done.6, bf16[1024,768]{1,0:T(8,128)(2,1)S(1)} %fusion.15), kind=kOutput, calls=%fused_computation.110 | convolution fusion | flops 6039797760 | bytes 21233664 | tf_op jit(solution)/shard_map/dot_general | solution.py:145
  356.6 201.8 %fusion = f32[64,768]{1,0:T(8,128)S(1)} fusion(f32[3840,768]{1,0:T(8,128)} %fusion.70), kind=kCustom, calls=%all-reduce-scatter | all-reduce-scatter fusion | flops 3145729 | bytes 11993600
  569.6 7.4 fusion.36
  578.4 4.3 concatenate.26
  584.2 323.5 %psum.14 = f32[32,128]{1,0:T(8,128)S(1)} all-reduce(f32[32,128]{1,0:T(8,128)S(1)} %fusion.60), channel_id=1, replica_groups=mesh['seq'=16,'col'=4,'batch'=2] {'seq','col'}, use_global_device_ids=true, to_apply=%region_7.8 | all-reduce | flops 4096 | bytes 32768 | tf_op jit(solution)/shard_map/psum | solution.py:157
  909.0 9.2 psum.15
  (120 shorter events, 42.3 us)
Async XLA Ops:
  7.2 22.7 %copy-start = (bf16[768,1536]{1,0:T(8,128)(2,1)S(1)}, bf16[768,1536]{1,0:T(8,128)(2,1)}, u32[]{:S(2)}) copy-start(bf16[768,1536]{1,0:T(8,128)(2,1)} %param.17) | copy-start | bytes 7077892
  7.2 96.2 %all-gather.2.cloned.1.call-start = ((), (), s32[]{:S(2)}) async-start(), calls=%async_computation.1 | async-start | bytes 1597440 | tf_op jit(solution)/shard_map/all_gather | solution.py:72
  11.8 4.7 collective-permute-start
  15.2 5.5 collective-permute-start.1
  16.5 4.9 slice-start
  17.3 4.2 slice-start.1
  17.4 4.1 copy-start.11
  21.5 8.4 copy-start.6
  21.5 9.0 copy-start.10
  21.5 81.9 %copy-start.5 = (bf16[1536,64]{0,1:T(8,128)(2,1)S(1)}, bf16[1536,64]{0,1:T(8,128)(2,1)}, u32[]{:S(2)}) copy-start(bf16[1536,64]{0,1:T(8,128)(2,1)} %param.19) | copy-start | bytes 589828
  29.9 75.9 %copy-start.4 = (bf16[1024,128]{1,0:T(8,128)(2,1)S(1)}, bf16[1024,128]{1,0:T(8,128)(2,1)}, u32[]{:S(2)}) copy-start(bf16[1024,128]{1,0:T(8,128)(2,1)} %param.20) | copy-start | bytes 786436
  31.2 304.1 %reduce-scatter.4.cloned.1.call-start = ((), (), s32[]{:S(2)}) async-start(), calls=%async_computation.2 | async-start | bytes 3194880 | tf_op jit(solution)/shard_map/reduce_scatter | solution.py:118
  109.5 11.1 %copy-start.1 = (f32[8,128,32,32]{1,3,2,0:T(8,128)S(1)}, f32[8,128,32,32]{1,3,2,0:T(8,128)}, u32[]{:S(2)}) copy-start(f32[8,128,32,32]{1,3,2,0:T(8,128)} %fusion.101) | copy-start | bytes 12582916 | tf_op jit(solution)/shard_map/while
  129.1 11.1 %copy-start.1 = (f32[8,128,32,32]{1,3,2,0:T(8,128)S(1)}, f32[8,128,32,32]{1,3,2,0:T(8,128)}, u32[]{:S(2)}) copy-start(f32[8,128,32,32]{1,3,2,0:T(8,128)} %fusion.101) | copy-start | bytes 12582916 | tf_op jit(solution)/shard_map/while
  148.7 11.1 %copy-start.1 = (f32[8,128,32,32]{1,3,2,0:T(8,128)S(1)}, f32[8,128,32,32]{1,3,2,0:T(8,128)}, u32[]{:S(2)}) copy-start(f32[8,128,32,32]{1,3,2,0:T(8,128)} %fusion.101) | copy-start | bytes 12582916 | tf_op jit(solution)/shard_map/while
  168.3 11.1 %copy-start.1 = (f32[8,128,32,32]{1,3,2,0:T(8,128)S(1)}, f32[8,128,32,32]{1,3,2,0:T(8,128)}, u32[]{:S(2)}) copy-start(f32[8,128,32,32]{1,3,2,0:T(8,128)} %fusion.101) | copy-start | bytes 12582916 | tf_op jit(solution)/shard_map/while
  342.7 12.6 %copy-start.2 = (bf16[1024,768]{1,0:T(8,128)(2,1)}, bf16[1024,768]{1,0:T(8,128)(2,1)S(1)}, u32[]{:S(2)}) copy-start(bf16[1024,768]{1,0:T(8,128)(2,1)S(1)} %fusion.15) | copy-start | bytes 4718596
  355.3 209.1 %collective-permute-start.2 = (bf16[2,768]{1,0:T(2,128)(2,1)S(1)}, bf16[2,768]{1,0:T(2,128)(2,1)S(1)}, u32[]{:S(2)}, u32[]{:S(2)}) collective-permute-start(bf16[2,768]{1,0:T(2,128)(2,1)S(1)} %get-tuple-element.104), channel_id=1, source_target_pairs={{2,0},{4,2},{6,4},{8,6},{10,8},{12,10},{14,12},{16,14},{18,16},{20... | collective-permute-start | bytes 9224 | tf_op jit(solution)/shard_map/ppermute | solution.py:23
  558.3 9.3 %copy-start.3 = (bf16[1024,768]{1,0:T(8,128)(2,1)S(1)}, bf16[1024,768]{1,0:T(8,128)(2,1)}, u32[]{:S(2)}) copy-start(bf16[1024,768]{1,0:T(8,128)(2,1)} %copy-done.2) | copy-start | bytes 4718596
  558.4 18.6 %collective-permute-start.4 = (f32[64,768]{1,0:T(8,128)S(1)}, f32[64,768]{1,0:T(8,128)S(1)}, u32[]{:S(2)}, u32[]{:S(2)}) collective-permute-start(f32[64,768]{1,0:T(8,128)S(1)} %fusion), channel_id=1, source_target_pairs={{0,2},{2,4},{4,6},{6,8},{8,10},{10,12},{12,14},{14,16},{16,18},{18... | collective-permute-start | bytes 589832
  559.8 17.2 %collective-permute-start.5 = (f32[64,768]{1,0:T(8,128)S(1)}, f32[64,768]{1,0:T(8,128)S(1)}, u32[]{:S(2)}, u32[]{:S(2)}) collective-permute-start(f32[64,768]{1,0:T(8,128)S(1)} %fusion), channel_id=1, source_target_pairs={{0,4},{2,6},{4,8},{6,10},{8,12},{10,14},{12,16},{14,18},{16,20},{1... | collective-permute-start | bytes 589832
  561.1 17.3 %collective-permute-start.6 = (f32[64,768]{1,0:T(8,128)S(1)}, f32[64,768]{1,0:T(8,128)}, u32[]{:S(2)}, u32[]{:S(2)}) collective-permute-start(f32[64,768]{1,0:T(8,128)S(1)} %fusion), channel_id=1, source_target_pairs={{0,6},{2,8},{4,10},{6,12},{8,14},{10,16},{12,18},{14,20},{16,22},{... | collective-permute-start | bytes 589832
  563.1 13.9 %collective-permute-start.7 = (f32[60,768]{1,0:T(8,128)S(1)}, f32[60,768]{1,0:T(8,128)S(1)}, u32[]{:S(2)}, u32[]{:S(2)}) collective-permute-start(f32[60,768]{1,0:T(8,128)S(1)} %slice.78), channel_id=1, source_target_pairs={{0,8},{2,10},{4,12},{6,14},{8,16},{10,18},{12,20},{14,22},{16,24},... | collective-permute-start | bytes 552968
  564.4 3.8 collective-permute-start.3
  (6 other events, 10.3 us)
Sparse Core Ops, SparseCore 0:
  31.3 72.0 all-gather.1
  189.8 145.4 reduce-scatter.3
where the time goes:
time: 927 us; the launch traced here: 926 us
  blocking collectives  535 us (58%)
  waiting for transfers between devices  219 us (24%)
  matrix products  118 us (13%)
  between operations  15.9 us (2%)
  starting transfers between devices  13.6 us (1%)
  other arithmetic  13 us (1%)
  local copies, waits for them, and re-layouts  11.9 us (1%)
    psum x1, blocking collectives, shards(): lax.psum(jnp.dot(member, projected, precision=highest), ('seq', 'col'))  324 us
    unnamed x1, blocking collectives  202 us
    reduce_scatter x1, waiting for transfers between devices, shards(): lax.psum_scatter(placed, ('seq', 'col'), scatter_dimension=0, tiled=True)  144 us
    all_gather x1, waiting for transfers between devices, shards(): every = lax.all_gather(normed, ('seq', 'col'), axis=0, tiled=True)  72 us
    dot_general x4, matrix products, pair_step(): jnp.einsum('ijkl,jl->ik', outer_grad, right_wide, precision=highest)  44.3 us
    dot_general x4, matrix products, pair_step(): jnp.einsum('ijkl,ik->jl', outer_grad, rows_left, precision=highest)  18.7 us
  transfers between devices with their start and end apart: 10, of which 3 were waited for; matrix products, arithmetic and copies ran while one was open for 23% of the time, Pallas kernels for 0%

commit v1 on v0

--- a/solution.py
+++ b/solution.py
@@ -154,7 +154,9 @@
     )
     projected = jnp.dot(share, projection, precision=highest)
     member = (labels[None, :] == jnp.arange(BUCKETS, dtype=jnp.int32)[:, None]).astype(jnp.float32)
-    sketch = lax.psum(jnp.dot(member, projected, precision=highest), ("seq", "col"))
+    sketch = jnp.sum(
+        lax.all_gather(jnp.dot(member, projected, precision=highest), ("seq", "col")), axis=0
+    )
     unit = sketch * lax.rsqrt(jnp.mean(sketch * sketch) + 1e-06)
     center = lax.psum(unit, "batch") / lax.axis_size("batch")
     return (input_grad[None], (unit - center)[None])

time: 927 us -> 663 us (0.72)
  blocking collectives: 535 us -> 210 us
  waiting for transfers between devices: 219 us -> 267 us
    psum x1 -> x0, blocking collectives: 324 us -> none  [shards(): lax.psum(jnp.dot(member, projected, precision=highest), ('seq', 'col'))]
    all_gather x0 -> x1, waiting for transfers between devices: none -> 48.3 us  [shards(): lax.all_gather(jnp.dot(member, projected, precision=highest), ('seq', 'co...]
  transfers between devices with their start and end apart: 10 -> 11, of which waited for: 3 -> 4; matrix products, arithmetic and copies ran while one was open for 23% -> 35% of each run, Pallas kernels for 0% -> 0%
where the time goes in v1:
time: 663 us; the launch traced here: 662 us
  waiting for transfers between devices  267 us (40%)
  blocking collectives  210 us (32%)
  matrix products  122 us (18%)
  other arithmetic  16.5 us (2%)
  local copies, waits for them, and re-layouts  16.4 us (2%)
  between operations  15.6 us (2%)
  starting transfers between devices  13.8 us (2%)
    unnamed x1, blocking collectives  202 us
    reduce_scatter x1, waiting for transfers between devices, shards(): lax.psum_scatter(placed, ('seq', 'col'), scatter_dimension=0, tiled=True)  143 us
    all_gather x1, waiting for transfers between devices, shards(): every = lax.all_gather(normed, ('seq', 'col'), axis=0, tiled=True)  72 us
    all_gather x1, waiting for transfers between devices, shards(): lax.all_gather(jnp.dot(member, projected, precision=highest), ('seq', 'co...  48.3 us
    dot_general x4, matrix products, pair_step(): jnp.einsum('ijkl,jl->ik', outer_grad, right_wide, precision=highest)  44.3 us
    dot_general x4, matrix products, pair_step(): jnp.einsum('ijkl,ik->jl', outer_grad, rows_left, precision=highest)  18.7 us
    dot_general x4, matrix products, pair_step(): lax.dot_general(block.reshape(bins_dev * col_len, pair_channels), out_wei...  14.5 us
  transfers between devices with their start and end apart: 11, of which 4 were waited for; matrix products, arithmetic and copies ran while one was open for 35% of the time, Pallas kernels for 0%

profile of v1, /device:TPU:8, one launch (start us, length us, event | category | flops | bytes accessed | tf_op | source)
XLA Modules:
  0.0 662.0 jit_solution(4628103828164114102)
XLA Ops:
  11.8 3.4 collective-permute-start
  21.5 8.4 %bitcast_reduce_fusion = (f32[8,768]{1,0:T(8,128)S(1)}, f32[1024,768]{1,0:T(8,128)}) fusion(f32[768]{0:T(1024)S(1)} %copy-done.13, bf16[1024,3840]{1,0:T(8,128)(2,1)S(1)} %fusion.34, bf16[3840,768]{1,0:T(8,128)(2,1)S(1)} %bitcast.120), kind=kOutput, calls=%fused_computation.26 | convolution fusion | flops 6047655936 | bytes 16935936 | tf_op jit(solution)/shard_map/dot_general | solution.py:59
  31.4 72.0 %all-gather.4.cloned.1.call-done = bf16[512,1536]{1,0:T(8,128)(2,1)} async-done(((bf16[8,1536]{1,0:T(8,128)(2,1)}), bf16[512,1536]{1,0:T(8,128)(2,1)}) %all-gather.4.cloned.1.call-update) | async-done | bytes 1572880 | tf_op jit(solution)/shard_map/all_gather | solution.py:72
  105.8 78.5 %while.13 = (s32[]{:T(128)}, f32[128,32]{1,0:T(8,128)S(1)}, f32[4,8,32]{2,1,0:T(8,128)S(1)}, bf16[4,8,128,128]{3,2,1,0:T(8,128)(2,1)}, bf16[1024,128]{1,0:T(8,12...) while((s32[]{:T(128)}, f32[128,32]{1,0:T(8,128)S(1)}, ...), condition=%wide.region_3.4_spmd.clone, body=%wide.region_2.3_spmd.clone.sunk | while | flops 293609472 | bytes 30050948 | solution.py:98
  105.8 3.6 fusion.101
  109.5 11.1 %fusion.102 = f32[1,8,32,1]{2,0,3,1:T(1,128)S(1)} fusion(f32[128,32,1,1]{0,2,1,3:T(1,128)S(1)} %copy.35, f32[8,128,32,32]{1,3,2,0:T(8,128)} %fusion.101), kind=kOutput, calls=%fused_computation.clone.1 | convolution fusion | flops 12582912 | bytes 4211712 | tf_op jit(solution)/shard_map/while/body/eval_jaxpr/ijkl,jl->ik/dot_general | solution.py:94
  120.6 4.7 fusion.103
  125.4 3.6 fusion.101
  129.1 11.1 %fusion.102 = f32[1,8,32,1]{2,0,3,1:T(1,128)S(1)} fusion(f32[128,32,1,1]{0,2,1,3:T(1,128)S(1)} %copy.35, f32[8,128,32,32]{1,3,2,0:T(8,128)} %fusion.101), kind=kOutput, calls=%fused_computation.clone.1 | convolution fusion | flops 12582912 | bytes 4211712 | tf_op jit(solution)/shard_map/while/body/eval_jaxpr/ijkl,jl->ik/dot_general | solution.py:94
  140.2 4.7 fusion.103
  145.0 3.6 fusion.101
  148.7 11.1 %fusion.102 = f32[1,8,32,1]{2,0,3,1:T(1,128)S(1)} fusion(f32[128,32,1,1]{0,2,1,3:T(1,128)S(1)} %copy.35, f32[8,128,32,32]{1,3,2,0:T(8,128)} %fusion.101), kind=kOutput, calls=%fused_computation.clone.1 | convolution fusion | flops 12582912 | bytes 4211712 | tf_op jit(solution)/shard_map/while/body/eval_jaxpr/ijkl,jl->ik/dot_general | solution.py:94
  159.8 4.7 fusion.103
  164.7 3.6 fusion.101
  168.3 11.1 %fusion.102 = f32[1,8,32,1]{2,0,3,1:T(1,128)S(1)} fusion(f32[128,32,1,1]{0,2,1,3:T(1,128)S(1)} %copy.35, f32[8,128,32,32]{1,3,2,0:T(8,128)} %fusion.101), kind=kOutput, calls=%fused_computation.clone.1 | convolution fusion | flops 12582912 | bytes 4211712 | tf_op jit(solution)/shard_map/while/body/eval_jaxpr/ijkl,jl->ik/dot_general | solution.py:94
  179.4 4.7 fusion.103
  192.0 143.4 %reduce-scatter.4.cloned.1.call-done = f32[8,1536]{1,0:T(8,128)} async-done(((f32[512,1536]{1,0:T(8,128)}), f32[8,1536]{1,0:T(8,128)}) %reduce-scatter.4.cloned.1.call-update) | async-done | bytes 49168 | tf_op jit(solution)/shard_map/reduce_scatter | solution.py:118
  339.1 3.7 fusion.15
  342.8 12.7 %fusion.70 = f32[3840,768]{1,0:T(8,128)} fusion(bf16[1024,3840]{1,0:T(8,128)(2,1)} %copy-done.7, bf16[1024,768]{1,0:T(8,128)(2,1)S(1)} %fusion.15), kind=kOutput, calls=%fused_computation.110 | convolution fusion | flops 6039797760 | bytes 21233664 | tf_op jit(solution)/shard_map/dot_general | solution.py:145
  356.7 202.0 %fusion = f32[64,768]{1,0:T(8,128)S(1)} fusion(f32[3840,768]{1,0:T(8,128)} %fusion.70), kind=kCustom, calls=%all-reduce-scatter | all-reduce-scatter fusion | flops 3145729 | bytes 11993600
  572.2 4.3 concatenate.26
  584.6 11.2 %fusion.36 = bf16[1,1024,768]{2,1,0:T(8,128)(2,1)} fusion(bf16[1024,5,768]{2,0,1:T(8,128)(2,1)} %fusion.31, bf16[5,768,768]{2,1,0:T(8,128)(2,1)} %bitcast.118), kind=kOutput, calls=%fused_computation.61 | convolution fusion | flops 6040584192 | bytes 15335424 | tf_op jit(solution)/shard_map/tko,kio->ti/dot_general | solution.py:137
  595.8 48.3 %all-gather.6.cloned.1.call-done = f32[2048,128]{1,0:T(8,128)} async-done(((f32[32,128]{1,0:T(8,128)}), f32[2048,128]{1,0:T(8,128)}) %all-gather.6.cloned.1.call-update) | async-done | bytes 1048592 | tf_op jit(solution)/shard_map/all_gather | solution.py:158
  646.8 8.1 %psum.7 = f32[32,128]{1,0:T(8,128)S(1)} all-reduce(f32[32,128]{1,0:T(8,128)S(1)} %broadcast_multiply_fusion), channel_id=1, replica_groups=mesh['seq'=16,'col'=4,'batch'=2] {'batch'}, use_global_device_ids=true, to_apply=%region_9.10 | all-reduce | flops 4096 | bytes 32768 | tf_op jit(solution)/shard_map/psum | solution.py:161
  (122 shorter events, 51.3 us)
Async XLA Ops:
  7.2 22.7 %copy-start = (bf16[768,1536]{1,0:T(8,128)(2,1)S(1)}, bf16[768,1536]{1,0:T(8,128)(2,1)}, u32[]{:S(2)}) copy-start(bf16[768,1536]{1,0:T(8,128)(2,1)} %param.17) | copy-start | bytes 7077892
  7.2 96.2 %all-gather.4.cloned.1.call-start = ((), (), s32[]{:S(2)}) async-start(), calls=%async_computation.1 | async-start | bytes 1597440 | tf_op jit(solution)/shard_map/all_gather | solution.py:72
  11.8 4.7 collective-permute-start
  15.2 5.5 collective-permute-start.1
  16.5 4.9 slice-start
  17.3 4.2 slice-start.1
  21.5 8.4 %copy-start.7 = (bf16[1024,3840]{1,0:T(8,128)(2,1)}, bf16[1024,3840]{1,0:T(8,128)(2,1)S(1)}, u32[]{:S(2)}) copy-start(bf16[1024,3840]{1,0:T(8,128)(2,1)S(1)} %fusion.34) | copy-start | bytes 23592964
  21.5 9.0 %copy-start.12 = (f32[1536]{0:T(1024)S(1)}, f32[1536]{0:T(1024)}, u32[]{:S(2)}) copy-start(f32[1536]{0:T(1024)} %param.18) | copy-start | bytes 18436
  21.5 81.9 %copy-start.6 = (bf16[1536,64]{0,1:T(8,128)(2,1)S(1)}, bf16[1536,64]{0,1:T(8,128)(2,1)}, u32[]{:S(2)}) copy-start(bf16[1536,64]{0,1:T(8,128)(2,1)} %param.19) | copy-start | bytes 589828
  29.9 75.9 %copy-start.5 = (bf16[1024,128]{1,0:T(8,128)(2,1)S(1)}, bf16[1024,128]{1,0:T(8,128)(2,1)}, u32[]{:S(2)}) copy-start(bf16[1024,128]{1,0:T(8,128)(2,1)} %param.20) | copy-start | bytes 786436
  31.2 304.2 %reduce-scatter.4.cloned.1.call-start = ((), (), s32[]{:S(2)}) async-start(), calls=%async_computation.2 | async-start | bytes 3194880 | tf_op jit(solution)/shard_map/reduce_scatter | solution.py:118
  109.5 11.1 %copy-start.1 = (f32[8,128,32,32]{1,3,2,0:T(8,128)S(1)}, f32[8,128,32,32]{1,3,2,0:T(8,128)}, u32[]{:S(2)}) copy-start(f32[8,128,32,32]{1,3,2,0:T(8,128)} %fusion.101) | copy-start | bytes 12582916 | tf_op jit(solution)/shard_map/while
  129.1 11.1 %copy-start.1 = (f32[8,128,32,32]{1,3,2,0:T(8,128)S(1)}, f32[8,128,32,32]{1,3,2,0:T(8,128)}, u32[]{:S(2)}) copy-start(f32[8,128,32,32]{1,3,2,0:T(8,128)} %fusion.101) | copy-start | bytes 12582916 | tf_op jit(solution)/shard_map/while
  148.7 11.1 %copy-start.1 = (f32[8,128,32,32]{1,3,2,0:T(8,128)S(1)}, f32[8,128,32,32]{1,3,2,0:T(8,128)}, u32[]{:S(2)}) copy-start(f32[8,128,32,32]{1,3,2,0:T(8,128)} %fusion.101) | copy-start | bytes 12582916 | tf_op jit(solution)/shard_map/while
  168.3 11.1 %copy-start.1 = (f32[8,128,32,32]{1,3,2,0:T(8,128)S(1)}, f32[8,128,32,32]{1,3,2,0:T(8,128)}, u32[]{:S(2)}) copy-start(f32[8,128,32,32]{1,3,2,0:T(8,128)} %fusion.101) | copy-start | bytes 12582916 | tf_op jit(solution)/shard_map/while
  189.7 454.4 %all-gather.6.cloned.1.call-start = ((), (), s32[]{:S(2)}) async-start(), calls=%async_computation.3 | async-start | bytes 1064960 | tf_op jit(solution)/shard_map/all_gather | solution.py:158
  342.7 12.7 %copy-start.2 = (bf16[1024,768]{1,0:T(8,128)(2,1)}, bf16[1024,768]{1,0:T(8,128)(2,1)S(1)}, u32[]{:S(2)}) copy-start(bf16[1024,768]{1,0:T(8,128)(2,1)S(1)} %fusion.15) | copy-start | bytes 4718596
  355.4 209.4 %collective-permute-start.2 = (bf16[2,768]{1,0:T(2,128)(2,1)S(1)}, bf16[2,768]{1,0:T(2,128)(2,1)S(1)}, u32[]{:S(2)}, u32[]{:S(2)}) collective-permute-start(bf16[2,768]{1,0:T(2,128)(2,1)S(1)} %get-tuple-element.104), channel_id=1, source_target_pairs={{2,0},{4,2},{6,4},{8,6},{10,8},{12,10},{14,12},{16,14},{18,16},{20... | collective-permute-start | bytes 9224 | tf_op jit(solution)/shard_map/ppermute | solution.py:23
  558.8 9.2 %copy-start.3 = (bf16[1024,768]{1,0:T(8,128)(2,1)S(1)}, bf16[1024,768]{1,0:T(8,128)(2,1)}, u32[]{:S(2)}) copy-start(bf16[1024,768]{1,0:T(8,128)(2,1)} %copy-done.2) | copy-start | bytes 4718596
  558.8 9.5 %collective-permute-start.4 = (f32[64,768]{1,0:T(8,128)S(1)}, f32[64,768]{1,0:T(8,128)S(1)}, u32[]{:S(2)}, u32[]{:S(2)}) collective-permute-start(f32[64,768]{1,0:T(8,128)S(1)} %fusion), channel_id=1, source_target_pairs={{0,2},{2,4},{4,6},{6,8},{8,10},{10,12},{12,14},{14,16},{16,18},{18... | collective-permute-start | bytes 589832
  560.2 8.1 %collective-permute-start.5 = (f32[64,768]{1,0:T(8,128)S(1)}, f32[64,768]{1,0:T(8,128)S(1)}, u32[]{:S(2)}, u32[]{:S(2)}) collective-permute-start(f32[64,768]{1,0:T(8,128)S(1)} %fusion), channel_id=1, source_target_pairs={{0,4},{2,6},{4,8},{6,10},{8,12},{10,14},{12,16},{14,18},{16,20},{1... | collective-permute-start | bytes 589832
  561.5 10.7 %collective-permute-start.6 = (f32[64,768]{1,0:T(8,128)S(1)}, f32[64,768]{1,0:T(8,128)}, u32[]{:S(2)}, u32[]{:S(2)}) collective-permute-start(f32[64,768]{1,0:T(8,128)S(1)} %fusion), channel_id=1, source_target_pairs={{0,6},{2,8},{4,10},{6,12},{8,14},{10,16},{12,18},{14,20},{16,22},{... | collective-permute-start | bytes 589832
  563.5 4.8 collective-permute-start.7
  564.8 16.6 %collective-permute-start.3 = (bf16[2,768]{1,0:T(2,128)(2,1)S(1)}, bf16[2,768]{1,0:T(2,128)(2,1)S(1)}, u32[]{:S(2)}, u32[]{:S(2)}) collective-permute-start(bf16[2,768]{1,0:T(2,128)(2,1)S(1)} %get-tuple-element.103), channel_id=1, source_target_pairs={{0,2},{2,4},{4,6},{6,8},{8,10},{10,12},{12,14},{14,16},{16,18},{18... | collective-permute-start | bytes 9224 | tf_op jit(solution)/shard_map/ppermute | solution.py:21
  (7 other events, 20.6 us)
Sparse Core Ops, SparseCore 0:
  31.3 72.0 all-gather.3
  189.8 145.5 reduce-scatter.3
  578.8 65.3 all-gather.5
